TPU v7x, 32 devices: a whole 2x2x4 slice. The times are simulated.
32 devices in a mesh: dp: 4 (over x, core), ctx: 4 (over z), tensor: 2 (over y).
Axes of the slice: x: 2, y: 2, z: 4, core: 2. Of those that a mesh axis runs over, the one named last changes fastest.
Arguments:
- inputs: bfloat16 [8192, 768], P(('dp', 'ctx')), may hold values from -6 to 6
- segments: int32 [4, 2048], P('dp', 'ctx'), may hold values from 0 to 7, never falling along the last dimension, each value on 1 to 1536 neighbouring positions
- query_proj: bfloat16 [768, 768], P(None, 'tensor'), may hold values from -0.4375 to 0.4375
- key_proj: bfloat16 [768, 768], P(None, 'tensor'), may hold values from -0.21875 to 0.21875
- value_proj: bfloat16 [768, 768], P(None, 'tensor'), may hold values from -0.21875 to 0.21875
- query_bias: bfloat16 [768], P('tensor'), may hold values from -3 to 3
- value_bias: bfloat16 [768], P('tensor'), may hold values from -0.59765625 to 0.59765625
- output_proj: bfloat16 [768, 768], P('tensor'), may hold values from -0.875 to 0.875
- output_bias: bfloat16 [768], replicated, may hold values from -1.1953125 to 1.1953125
- attn_gain: bfloat16 [768], replicated, may hold values from 0.5 to 1.5
- attn_shift: bfloat16 [768], replicated, may hold values from -1.1953125 to 1.1953125
- expand_proj: bfloat16 [768, 3072], P(None, 'tensor'), may hold values from -0.21875 to 0.21875
- expand_bias: bfloat16 [3072], P('tensor'), may hold values from -3 to 3
- shrink_proj: bfloat16 [3072, 768], P('tensor'), may hold values from -0.109375 to 0.109375
- shrink_bias: bfloat16 [768], replicated, may hold values from -1.1953125 to 1.1953125
- final_gain: bfloat16 [768], replicated, may hold values from 0.5 to 1.5
- final_shift: bfloat16 [768], replicated, may hold values from -1.1953125 to 1.1953125
- cotangent: bfloat16 [8192, 768], P(('dp', 'ctx')), may hold values from -6 to 6
Outputs:
- output: bfloat16 [8192, 768], P(('dp', 'ctx'))
- input_grad: float32 [8192, 768], P(('dp', 'ctx'))
- query_grad: float32 [768, 768], P(None, 'tensor')
- key_grad: float32 [768, 768], P(None, 'tensor')
- value_grad: float32 [768, 768], P(None, 'tensor')
- qbias_grad: float32 [768], P('tensor')
- vbias_grad: float32 [768], P('tensor')
- oproj_grad: float32 [768, 768], P('tensor')
- obias_grad: float32 [768], replicated
- again_grad: float32 [768], replicated
- ashift_grad: float32 [768], replicated
- expand_grad: float32 [768, 3072], P(None, 'tensor')
- ebias_grad: float32 [3072], P('tensor')
- shrink_grad: float32 [3072, 768], P('tensor')
- sbias_grad: float32 [768], replicated
- fgain_grad: float32 [768], replicated
- fshift_grad: float32 [768], replicated
Inputs may be any that keep to these rules, and one draw needn't show every extreme that they name: `segments`: along each sequence the ids never fall; every id from 0 to 7 names one document of the sequence, and one document has 1536 tokens.
All inputs are finite; a program needn't handle non-finite values.
Results may differ from a plain program's by a relative error of at most 0.019.
Values may be sent and summed in bfloat16 or wider, within the bound.
A program may use at most 256 MiB of HBM per device.

v0:
```python
import jax
import jax.numpy as jnp
from jax import lax
from jax.sharding import PartitionSpec as P

HEAD_DIM = 64
norm_eps = 1e-12
masked = -1e30
contract_rows = (((0,), (0,)), ((), ()))
contract_cols = (((1,), (1,)), ((), ()))


def matmul(left, right):
    return jnp.dot(left, right, preferred_element_type=jnp.float32)


def inner_rows(left, right):
    return lax.dot_general(left, right, contract_rows, preferred_element_type=jnp.float32)


def inner_cols(left, right):
    return lax.dot_general(left, right, contract_cols, preferred_element_type=jnp.float32)


def norm_forward(values, gain, shift):
    centred = values - jnp.mean(values, axis=-1, keepdims=True)
    spread = jnp.mean(centred * centred, axis=-1, keepdims=True)
    recip = lax.rsqrt(spread + norm_eps)
    normed = centred * recip
    return (normed * gain + shift, normed, recip)


def norm_backward(upstream, normed, recip, gain):
    scaled = upstream * gain
    centred = (
        scaled
        - jnp.mean(scaled, axis=-1, keepdims=True)
        - normed * jnp.mean(scaled * normed, axis=-1, keepdims=True)
    )
    return (centred * recip, jnp.sum(upstream * normed, axis=0), jnp.sum(upstream, axis=0))


def cross_scores(left, right):
    return inner_cols(left, right)


def spread_apply(weights_in, right):
    return matmul(weights_in, right)


def spread_transpose(weights_in, left):
    return inner_rows(weights_in, left)


def body(
    inputs,
    segments,
    query_proj,
    key_proj,
    value_proj,
    query_bias,
    value_bias,
    output_proj,
    output_bias,
    attn_gain,
    attn_shift,
    expand_proj,
    expand_bias,
    shrink_proj,
    shrink_bias,
    final_gain,
    final_shift,
    cotangent,
):
    head_count = query_proj.shape[1] // HEAD_DIM
    scale = HEAD_DIM ** (-0.5)
    seg_local = segments[0]
    queries = (matmul(inputs, query_proj) + query_bias.astype(jnp.float32)).astype(jnp.bfloat16)
    keys = matmul(inputs, key_proj).astype(jnp.bfloat16)
    values = (matmul(inputs, value_proj) + value_bias.astype(jnp.float32)).astype(jnp.bfloat16)
    all_keys, all_values, key_ids = (
        lax.all_gather(keys, "ctx", axis=0, tiled=True),
        lax.all_gather(values, "ctx", axis=0, tiled=True),
        lax.all_gather(seg_local.astype(jnp.bfloat16), "ctx", axis=0, tiled=True),
    )
    query_segs = seg_local.astype(jnp.float32)
    key_segs = key_ids.astype(jnp.float32)
    same_seg = query_segs[:, None] == key_segs[None, :]

    def split_heads(matrix):
        return jnp.swapaxes(matrix.reshape(matrix.shape[0], head_count, HEAD_DIM), 0, 1)

    def join_heads(stack):
        return jnp.swapaxes(stack, 0, 1).reshape(stack.shape[1], head_count * HEAD_DIM)

    query_heads = split_heads(queries)
    key_heads = split_heads(all_keys)
    value_heads = split_heads(all_values)

    def head_forward(state, triple):
        query_head, key_head, value_head = triple
        scores = cross_scores(query_head, key_head) * scale
        scores = jnp.where(same_seg, scores, masked)
        row_max = jnp.max(scores, axis=1, keepdims=True)
        exp_scores = jnp.where(same_seg, jnp.exp(scores - row_max), 0.0)
        row_sum = jnp.sum(exp_scores, axis=1, keepdims=True)
        attn_probs = (exp_scores / row_sum).astype(jnp.bfloat16)
        mixed = spread_apply(attn_probs, value_head)
        return (state, (mixed, row_max + jnp.log(row_sum)))

    mixed_heads, log_sums = lax.scan(head_forward, None, (query_heads, key_heads, value_heads))[1]
    attended = join_heads(mixed_heads).astype(jnp.bfloat16)
    attn_total = lax.psum(matmul(attended, output_proj).astype(jnp.bfloat16), "tensor").astype(
        jnp.float32
    )
    attn_gain_f = attn_gain.astype(jnp.float32)
    first, first_normed, first_recip = norm_forward(
        inputs.astype(jnp.float32) + attn_total + output_bias.astype(jnp.float32),
        attn_gain_f,
        attn_shift.astype(jnp.float32),
    )
    first_low = first.astype(jnp.bfloat16)
    pre_act = matmul(first_low, expand_proj) + expand_bias.astype(jnp.float32)
    activated, gelu_back = jax.vjp(lambda pre_in: jax.nn.gelu(pre_in, approximate=False), pre_act)
    hidden = activated.astype(jnp.bfloat16)
    feed_total = lax.psum(matmul(hidden, shrink_proj).astype(jnp.bfloat16), "tensor").astype(
        jnp.float32
    )
    second = first + feed_total + shrink_bias.astype(jnp.float32)
    final_gain_f = final_gain.astype(jnp.float32)
    output, second_normed, second_recip = norm_forward(
        second, final_gain_f, final_shift.astype(jnp.float32)
    )
    upstream = cotangent.astype(jnp.float32)
    grad_second, fgain_grad, fshift_grad = norm_backward(
        upstream, second_normed, second_recip, final_gain_f
    )
    sbias_grad = jnp.sum(grad_second, axis=0)
    grad_second_low = grad_second.astype(jnp.bfloat16)
    shrink_grad = inner_rows(hidden, grad_second_low)
    grad_act = inner_cols(grad_second_low, shrink_proj)
    grad_pre = gelu_back(grad_act)[0].astype(jnp.bfloat16)
    ebias_grad = jnp.sum(grad_pre.astype(jnp.float32), axis=0)
    expand_grad = inner_rows(first_low, grad_pre)
    grad_first = grad_second + lax.psum(
        inner_cols(grad_pre, expand_proj).astype(jnp.bfloat16), "tensor"
    ).astype(jnp.float32)
    grad_mix, again_grad, ashift_grad = norm_backward(
        grad_first, first_normed, first_recip, attn_gain_f
    )
    obias_grad = jnp.sum(grad_mix, axis=0)
    grad_mix_low = grad_mix.astype(jnp.bfloat16)
    oproj_grad = inner_rows(attended, grad_mix_low)
    grad_attended = inner_cols(grad_mix_low, output_proj).astype(jnp.bfloat16)
    grad_heads = split_heads(grad_attended)

    def head_backward(state, group):
        query_head, key_head, value_head, grad_head, log_sum = group
        scores = cross_scores(query_head, key_head) * scale
        attn_probs = jnp.where(same_seg, jnp.exp(scores - log_sum), 0.0)
        grad_probs = cross_scores(grad_head, value_head)
        row_dot = jnp.sum(attn_probs * grad_probs, axis=1, keepdims=True)
        grad_scores = (attn_probs * (grad_probs - row_dot)).astype(jnp.bfloat16)
        grad_query = spread_apply(grad_scores, key_head) * scale
        grad_key = spread_transpose(grad_scores, query_head) * scale
        grad_value = spread_transpose(attn_probs.astype(jnp.bfloat16), grad_head)
        return (state, (grad_query, grad_key, grad_value))

    query_back, key_back, value_back = lax.scan(
        head_backward, None, (query_heads, key_heads, value_heads, grad_heads, log_sums)
    )[1]
    grad_queries = join_heads(query_back).astype(jnp.bfloat16)
    key_sum, value_sum = (
        lax.psum_scatter(
            join_heads(key_back).astype(jnp.bfloat16), "ctx", scatter_dimension=0, tiled=True
        ).astype(jnp.float32),
        lax.psum_scatter(
            join_heads(value_back).astype(jnp.bfloat16), "ctx", scatter_dimension=0, tiled=True
        ).astype(jnp.float32),
    )
    grad_keys = key_sum.astype(jnp.bfloat16)
    grad_values = value_sum.astype(jnp.bfloat16)
    qbias_grad = jnp.sum(grad_queries.astype(jnp.float32), axis=0)
    vbias_grad = jnp.sum(grad_values.astype(jnp.float32), axis=0)
    query_grad = inner_rows(inputs, grad_queries)
    key_grad = inner_rows(inputs, grad_keys)
    value_grad = inner_rows(inputs, grad_values)
    back_terms = (
        inner_cols(grad_queries, query_proj)
        + inner_cols(grad_keys, key_proj)
        + inner_cols(grad_values, value_proj)
    )
    input_grad = grad_mix + lax.psum(back_terms.astype(jnp.bfloat16), "tensor").astype(jnp.float32)
    (
        query_grad,
        key_grad,
        value_grad,
        qbias_grad,
        vbias_grad,
        oproj_grad,
        obias_grad,
        again_grad,
        ashift_grad,
        expand_grad,
        ebias_grad,
        shrink_grad,
        sbias_grad,
        fgain_grad,
        fshift_grad,
    ) = lax.psum(
        (
            query_grad,
            key_grad,
            value_grad,
            qbias_grad,
            vbias_grad,
            oproj_grad,
            obias_grad,
            again_grad,
            ashift_grad,
            expand_grad,
            ebias_grad,
            shrink_grad,
            sbias_grad,
            fgain_grad,
            fshift_grad,
        ),
        ("dp", "ctx"),
    )
    return (
        output.astype(jnp.bfloat16),
        input_grad,
        query_grad,
        key_grad,
        value_grad,
        qbias_grad,
        vbias_grad,
        oproj_grad,
        obias_grad,
        again_grad,
        ashift_grad,
        expand_grad,
        ebias_grad,
        shrink_grad,
        sbias_grad,
        fgain_grad,
        fshift_grad,
    )


def solution(mesh):
    in_specs = (
        P(("dp", "ctx"), None),
        P("dp", "ctx"),
        P(None, "tensor"),
        P(None, "tensor"),
        P(None, "tensor"),
        P("tensor"),
        P("tensor"),
        P("tensor", None),
        P(),
        P(),
        P(),
        P(None, "tensor"),
        P("tensor"),
        P("tensor", None),
        P(),
        P(),
        P(),
        P(("dp", "ctx"), None),
    )
    out_specs = (
        P(("dp", "ctx"), None),
        P(("dp", "ctx"), None),
        P(None, "tensor"),
        P(None, "tensor"),
        P(None, "tensor"),
        P("tensor"),
        P("tensor"),
        P("tensor", None),
        P(),
        P(),
        P(),
        P(None, "tensor"),
        P("tensor"),
        P("tensor", None),
        P(),
        P(),
        P(),
    )
    return jax.shard_map(body, mesh=mesh, in_specs=in_specs, out_specs=out_specs, check_vma=False)
```

profile of v0, /device:TPU:0, one launch (start us, length us, event | category | flops | bytes accessed | tf_op | source)
XLA Modules:
  0.0 743.4 jit_solution(2113761524882374570)
XLA Ops:
  7.3 2.8 convolution_convert_fusion.4
  10.2 2.4 fusion.62
  12.7 13.7 %all-gather = bf16[1,2048]{1,0:T(2,128)(2,1)S(1)} all-gather(bf16[1,512]{1,0:T(2,128)(2,1)S(1)} %get-tuple-element.288), channel_id=2, replica_groups=mesh['dp'=4,'ctx'=4,'tensor'=2] {'ctx'}, dimensions={1}, use_global_device_ids=true | all-gather | bytes 5120 | tf_op jit(solution)/shard_map/all_gather | solution.py:84
  29.1 21.0 %all-gather.4.cloned.1.call-done = bf16[2048,384]{1,0:T(8,128)(2,1)} async-done(((bf16[512,384]{1,0:T(8,128)(2,1)}), bf16[2048,384]{1,0:T(8,128)(2,1)}) %all-gather.4.cloned.1.call-update) | async-done | bytes 1572880 | tf_op jit(solution)/shard_map/all_gather | solution.py:82
  50.1 2.6 copy.43
  52.6 4.1 copy.45
  56.8 31.5 %all-gather.6.cloned.1.call-done = bf16[2048,384]{1,0:T(8,128)(2,1)} async-done(((bf16[512,384]{1,0:T(8,128)(2,1)}), bf16[2048,384]{1,0:T(8,128)(2,1)}) %all-gather.6.cloned.1.call-update) | async-done | bytes 1572880 | tf_op jit(solution)/shard_map/all_gather | solution.py:83
  88.2 2.6 copy.44
  90.8 4.1 copy.46
  94.9 38.4 %while.28 = (s32[]{:T(128)}, bf16[6,512,64]{1,2,0:T(8,128)(2,1)S(1)}, f32[6,512,1]{1,2,0:T(1,128)}, bf16[6,512,64]{2,1,0:T(8,128)(2,1)}, bf16[6,2048,64]{2,1,0:T...) while((s32[]{:T(128)}, ...), condition=%wide.region_3.4_spmd.clone, body=%wide.region_0.3_spmd.clone.sunk | while | flops 286260736 | bytes 13946985 | solution.py:111
  94.9 2.0 fusion.132
  98.1 2.6 fusion.134
  101.3 2.0 fusion.132
  104.5 2.6 fusion.134
  107.7 2.0 fusion.132
  110.9 2.6 fusion.134
  114.1 2.0 fusion.132
  117.3 2.6 fusion.134
  120.5 2.0 fusion.132
  123.7 2.6 fusion.134
  126.9 2.0 fusion.132
  130.1 2.6 fusion.134
  133.3 2.7 convolution_convert_fusion.2
  140.6 28.8 %all-reduce.8.cloned.1.call-done = bf16[512,768]{1,0:T(8,128)(2,1)} async-done(((bf16[512,768]{1,0:T(8,128)(2,1)}), bf16[512,768]{1,0:T(8,128)(2,1)}) %all-reduce.8.cloned.1.call-update) | async-done | bytes 786448 | tf_op jit(solution)/shard_map/psum | solution.py:113
  171.5 9.5 %multiply_convert_fusion.1 = (bf16[512,1536]{1,0:T(8,128)(2,1)S(1)}, f32[512,1536]{1,0:T(8,128)}, f32[512,1536]{1,0:T(8,128)}) fusion(f32[1536]{0:T(1024)S(1)} %copy-done.41, bf16[768,1536]{1,0:T(8,128)(2,1)S(1)} %copy-done, f32[768]{0:T(1024)S(1)} %copy-done.38, f32[768]{0:T(1024)S(1)} %copy-done.23, f32[512]{0:T(512)S(1)} %add_rsqrt_fusion.1, ...), kind=kOutput, calls=%fused_computation.62 | convolution fusion | flops 1263403008 | bytes 11815936 | tf_op jit(solution)/shard_map/dot_general | solution.py:14
  182.3 2.3 convolution_convert_fusion.1
  184.8 34.2 %all-reduce.10.cloned.1.call-done = bf16[512,768]{1,0:T(8,128)(2,1)} async-done(((bf16[512,768]{1,0:T(8,128)(2,1)}), bf16[512,768]{1,0:T(8,128)(2,1)}) %all-reduce.10.cloned.1.call-update) | async-done | bytes 786448 | tf_op jit(solution)/shard_map/psum | solution.py:126
  219.1 2.2 fusion.78
  225.0 2.9 convert_reduce_fusion
  229.1 2.3 convolution_convert_fusion
  231.5 34.4 %all-reduce.12.cloned.1.call-done = bf16[512,768]{1,0:T(8,128)(2,1)} async-done(((bf16[512,768]{1,0:T(8,128)(2,1)}), bf16[512,768]{1,0:T(8,128)(2,1)}) %all-reduce.12.cloned.1.call-update) | async-done | bytes 786448 | tf_op jit(solution)/shard_map/psum | solution.py:145
  265.9 3.5 multiply_reduce_fusion.1
  273.7 70.0 %while.29 = (s32[]{:T(128)}, bf16[6,512,64]{1,2,0:T(8,128)(2,1)S(1)}, bf16[6,2048,64]{1,2,0:T(8,128)(2,1)}, bf16[6,2048,64]{1,2,0:T(8,128)(2,1)}, bf16[6,512,64]...) while((s32[]{:T(128)}, ...), condition=%wide.region_17.18_spmd.clone, body=%wide.region_15.17_spmd.clone.sunk | while | flops 681737728 | bytes 34759808 | solution.py:169
  276.2 2.6 multiply_reduce_fusion.7
  279.3 2.1 fusion.146
  283.2 2.2 fusion.145
  287.9 2.6 multiply_reduce_fusion.7
  290.9 2.2 fusion.146
  294.9 2.1 fusion.145
  299.5 2.6 multiply_reduce_fusion.7
  302.6 2.2 fusion.146
  306.6 2.1 fusion.145
  311.2 2.6 multiply_reduce_fusion.7
  314.3 2.2 fusion.146
  318.2 2.1 fusion.145
  322.9 2.6 multiply_reduce_fusion.7
  325.9 2.2 fusion.146
  329.9 2.1 fusion.145
  334.5 2.6 multiply_reduce_fusion.7
  337.6 2.1 fusion.146
  341.5 2.1 fusion.145
  345.1 5.1 fusion.67
  350.3 3.8 fusion.73
  357.4 21.8 %reduce-scatter.3.cloned.1.call-done = bf16[512,384]{0,1:T(8,128)(2,1)} async-done(((bf16[2048,384]{0,1:T(8,128)(2,1)}), bf16[512,384]{0,1:T(8,128)(2,1)}) %reduce-scatter.3.cloned.1.call-update) | async-done | bytes 393232 | tf_op jit(solution)/shard_map/reduce_scatter | solution.py:174
  379.1 3.0 fusion.82
  382.1 33.8 %reduce-scatter.5.cloned.1.call-done = bf16[512,384]{0,1:T(8,128)(2,1)} async-done(((bf16[2048,384]{0,1:T(8,128)(2,1)}), bf16[512,384]{0,1:T(8,128)(2,1)}) %reduce-scatter.5.cloned.1.call-update) | async-done | bytes 393232 | tf_op jit(solution)/shard_map/reduce_scatter | solution.py:177
  415.8 3.5 add_convert_fusion.1
  424.7 61.2 %all-reduce = (f32[384]{0:T(512)}, f32[384]{0:T(512)}, f32[768]{0:T(1024)}, f32[768]{0:T(1024)}, f32[768]{0:T(1024)}, /*index=5*/f32[1536]{0:T(1024)}, f32[768]{0:T(1024)}, f32[768]{0:T(1024)}, f32[768]{0:T(1024)}) all-reduce(f32[384]{0:T(512)S(1)} %reduce_sum.182, ...), channel_id=1, replica_groups=mesh['dp'=4,'ctx'=4,'tensor'=2] {'dp','ctx'}, use_global_device_ids=true, to_apply=%region_25.26 | all-reduce | flops 6912 | bytes 55296 | tf_op jit(solution)/shard_map/psum | solution.py:210
  485.9 2.4 convert_add_fusion
  488.3 231.7 %all-reduce.16.cloned.1.call-done = (f32[768,384]{0,1:T(8,128)}, f32[768,384]{0,1:T(8,128)}, f32[768,384]{0,1:T(8,128)}, f32[384,768]{1,0:T(8,128)}, f32[768,1536]{1,0:T(8,128)}, /*index=5*/f32[1536,768]{1,0:T(8,128)}) async-done(((f32[768,384]{0,1:T(8,128)}, f32[768,384]{0,1:T(8,128)}, f32[768,384]{0,1:T(8,128)}, f32[384,768]{1,0:T(8,128)}, f32[768,1536]{1,0:T(8,128)}, /*index=5*/f32[1536,768]{1,0:T(8,128)}), ...) | async-done | bytes 14155792 | tf_op jit(solution)/shard_map/psum | solution.py:210
  720.1 2.7 copy.50
  722.8 2.7 copy.51
  728.0 5.5 copy.92
  733.5 2.4 copy.93
  (219 shorter events, 72.9 us)
Async XLA Ops:
  7.2 164.2 %copy-start = (bf16[768,1536]{1,0:T(8,128)(2,1)S(1)}, bf16[768,1536]{1,0:T(8,128)(2,1)}, u32[]{:S(2)}) copy-start(bf16[768,1536]{1,0:T(8,128)(2,1)} %param.33) | copy-start | bytes 7077892
  7.2 3.0 copy-start.2
  7.2 2.9 copy-start.47
  7.2 5.4 copy-start.48
  7.2 5.4 copy-start.43
  7.2 42.8 %all-gather.4.cloned.1.call-start = ((), (), s32[]{:S(2)}) async-start(), calls=%async_computation.2 | async-start | bytes 1966080 | tf_op jit(solution)/shard_map/all_gather | solution.py:82
  10.1 78.1 %all-gather.6.cloned.1.call-start = ((), (), s32[]{:S(2)}) async-start(), calls=%async_computation.3 | async-start | bytes 1966080 | tf_op jit(solution)/shard_map/all_gather | solution.py:83
  12.6 156.8 %all-reduce.8.cloned.1.call-start = ((), (), s32[]{:S(2)}) async-start(), calls=%async_computation.4 | async-start | bytes 1572864 | tf_op jit(solution)/shard_map/psum | solution.py:113
  133.3 38.1 %copy-start.12 = (bf16[6,512,64]{1,2,0:T(8,128)(2,1)}, bf16[6,512,64]{1,2,0:T(8,128)(2,1)S(1)}, u32[]{:S(2)}) copy-start(bf16[6,512,64]{1,2,0:T(8,128)(2,1)S(1)} %get-tuple-element.109) | copy-start | bytes 1179652
  136.0 83.0 %all-reduce.10.cloned.1.call-start = ((), (), s32[]{:S(2)}) async-start(), calls=%async_computation.5 | async-start | bytes 1572864 | tf_op jit(solution)/shard_map/psum | solution.py:126
  169.4 1.6 copy-start.8
  169.4 2.1 copy-start.23
  169.4 2.1 copy-start.38
  169.4 2.1 copy-start.41
  170.9 10.1 %copy-start.26 = (f32[512]{0:T(512)}, f32[512]{0:T(512)S(1)}, u32[]{:S(2)}) copy-start(f32[512]{0:T(512)S(1)} %broadcast_multiply_fusion.5) | copy-start | bytes 6148
  171.5 9.6 %copy-start.29 = (f32[512]{0:T(512)}, f32[512]{0:T(512)S(1)}, u32[]{:S(2)}) copy-start(f32[512]{0:T(512)S(1)} %add_rsqrt_fusion.1) | copy-start | bytes 6148
  171.5 10.7 %copy-start.49 = (bf16[1536,768]{1,0:T(8,128)(2,1)S(1)}, bf16[1536,768]{1,0:T(8,128)(2,1)}, u32[]{:S(2)}) copy-start(bf16[1536,768]{1,0:T(8,128)(2,1)} %param.35) | copy-start | bytes 7077892
  181.0 1.2 copy-start.16
  182.2 2.6 copy-start.44
  182.2 2.6 copy-start.45
  182.2 2.6 copy-start.46
  182.2 36.8 %copy-start.24 = (f32[768]{0:T(1024)S(1)}, f32[768]{0:T(1024)}, u32[]{:S(2)}) copy-start(f32[768]{0:T(1024)} %convert_element_type.185) | copy-start | bytes 9220
  182.2 36.8 %copy-start.27 = (f32[512]{0:T(512)S(1)}, f32[512]{0:T(512)}, u32[]{:S(2)}) copy-start(f32[512]{0:T(512)} %copy-done.26) | copy-start | bytes 6148
  182.2 36.8 %copy-start.30 = (f32[512]{0:T(512)S(1)}, f32[512]{0:T(512)}, u32[]{:S(2)}) copy-start(f32[512]{0:T(512)} %copy-done.29) | copy-start | bytes 6148
  182.2 36.8 %copy-start.39 = (f32[768]{0:T(1024)S(1)}, f32[768]{0:T(1024)}, u32[]{:S(2)}) copy-start(f32[768]{0:T(1024)} %convert_element_type.186) | copy-start | bytes 9220
  184.5 81.4 %all-reduce.12.cloned.1.call-start = ((), (), s32[]{:S(2)}) async-start(), calls=%async_computation.6 | async-start | bytes 1572864 | tf_op jit(solution)/shard_map/psum | solution.py:145
  219.0 2.6 copy-start.14
  221.3 3.4 copy-start.54
  221.6 3.1 copy-start.53
  223.0 2.1 copy-start.50
  224.7 3.2 copy-start.3
  227.9 1.2 copy-start.51
  231.4 38.0 %copy-start.4 = (f32[512,768]{1,0:T(8,128)S(1)}, f32[512,768]{1,0:T(8,128)}, u32[]{:S(2)}) copy-start(f32[512,768]{1,0:T(8,128)} %copy-done.3) | copy-start | bytes 4718596
  231.4 38.0 %copy-start.9 = (bf16[512,768]{1,0:T(8,128)(2,1)S(1)}, bf16[512,768]{1,0:T(8,128)(2,1)}, u32[]{:S(2)}) copy-start(bf16[512,768]{1,0:T(8,128)(2,1)} %all-reduce.8.cloned.1.call-done) | copy-start | bytes 2359300
  231.4 147.7 %reduce-scatter.3.cloned.1.call-start = ((), (), s32[]{:S(2)}) async-start(), calls=%async_computation.7 | async-start | bytes 1966080 | tf_op jit(solution)/shard_map/reduce_scatter | solution.py:174
  265.9 3.6 copy-start.15
  269.5 2.5 copy-start.17
  270.8 1.1 copy-start.6
  343.7 1.4 copy-start.5
  343.7 72.2 %reduce-scatter.5.cloned.1.call-start = ((), (), s32[]{:S(2)}) async-start(), calls=%async_computation.8 | async-start | bytes 1966080 | tf_op jit(solution)/shard_map/reduce_scatter | solution.py:177
  344.4 5.8 copy-start.10
  344.4 5.8 copy-start.25
  344.5 5.8 copy-start.28
  344.5 5.7 copy-start.31
  344.5 141.4 %all-reduce.14.cloned.1.call-start = ((), (), s32[]{:S(2)}) async-start(), calls=%async_computation.9 | async-start | bytes 1572864 | tf_op jit(solution)/shard_map/psum | solution.py:193
  345.1 5.2 copy-start.40
  345.1 5.2 copy-start.52
  350.2 3.9 copy-start.22
  354.1 1.8 copy-start.7
  354.1 1.8 copy-start.13
  357.4 58.5 %copy-start.21 = (bf16[768,384]{1,0:T(8,128)(2,1)S(1)}, bf16[768,384]{1,0:T(8,128)(2,1)}, u32[]{:S(2)}) copy-start(bf16[768,384]{1,0:T(8,128)(2,1)} %param.26) | copy-start | bytes 1769476
  419.4 1.6 copy-start.11
  419.4 3.0 copy-start.18
  419.4 300.7 %all-reduce.16.cloned.1.call-start = ((), (), s32[]{:S(2)}) async-start(), calls=%async_computation.10 | async-start | bytes 28311552 | tf_op jit(solution)/shard_map/psum | solution.py:210
  423.9 0.7 copy-start.34
  423.9 0.7 copy-start.35
  423.9 0.7 copy-start.36
  423.9 0.7 copy-start.37
  423.9 0.7 copy-start.42
  720.1 5.5 copy-start.20
  722.8 4.1 copy-start.19
  727.0 6.5 slice-start
  728.0 5.5 slice-start.1
  733.5 3.4 copy-start.1
  (2 other events, 1.4 us)
Sparse Core Ops, SparseCore 0:
  10.2 39.8 all-gather.3
  52.2 35.9 all-gather.5
  136.1 33.1 all-reduce.7
  184.7 34.3 all-reduce.9
  231.5 34.3 all-reduce.11
  343.8 35.2 reduce-scatter.2
  381.5 34.2 reduce-scatter.4
  419.5 33.2 all-reduce.13
  459.1 260.8 all-reduce.15
where the time goes:
time: 746 us; the launch traced here: 743 us
  waiting for transfers between devices  438 us (59%)
  matrix products  141 us (19%)
  blocking collectives  74.9 us (10%)
  local copies, waits for them, and re-layouts  44.8 us (6%)
  other arithmetic  29.9 us (4%)
  between operations  14.4 us (2%)
    psum x1, waiting for transfers between devices, body(): lax.psum((query_grad, key_grad, value_grad, qbias_grad, vbias_grad, oproj...  232 us
    psum x1, blocking collectives, body(): lax.psum((query_grad, key_grad, value_grad, qbias_grad, vbias_grad, oproj...  61.2 us
    dot_general x24, matrix products, inner_cols(): lax.dot_general(left, right, contract_cols, preferred_element_type=jnp.fl...  52.3 us
    dot_general x18, matrix products, matmul(): return jnp.dot(left, right, preferred_element_type=jnp.float32)  47.6 us
    dot_general x18, matrix products, inner_rows(): lax.dot_general(left, right, contract_rows, preferred_element_type=jnp.fl...  40.7 us
    psum x1, waiting for transfers between devices, body(): lax.psum(inner_cols(grad_pre, expand_proj).astype(jnp.bfloat16), 'tensor')  34.4 us
    psum x1, waiting for transfers between devices, body(): lax.psum(matmul(hidden, shrink_proj).astype(jnp.bfloat16), 'tensor')  34.2 us
    reduce_scatter x1, waiting for transfers between devices, body(): lax.psum_scatter(join_heads(value_back).astype(jnp.bfloat16), 'ctx', scat...  33.8 us
  transfers between devices with their start and end apart: 9, of which 8 were waited for; matrix products, arithmetic and copies ran while one was open for 5% of the time, Pallas kernels for 0%

commit v1 on v0

--- a/solution.py
+++ b/solution.py
@@ -8,6 +8,36 @@
 masked = -1e30
 contract_rows = (((0,), (0,)), ((), ()))
 contract_cols = (((1,), (1,)), ((), ()))
+
+
+def _update_halves(inner_x, in_dim):
+    r2 = list(inner_x.shape[1:])
+    r2[in_dim] *= inner_x.shape[0]
+    return jnp.moveaxis(inner_x, 0, in_dim).reshape(r2)
+
+
+def turn_knots_on_mesh(local_x, row_axis, ndim_at):
+    p_count = jax.lax.axis_size(row_axis)
+    views = []
+    for t in range(p_count):
+        views.append((t, (t + 1) % p_count))
+    row_list = []
+    for p, kk in views:
+        row_list.append((kk, p))
+    current_value, next_value = ([], [])
+    for w in range(p_count - 1):
+        if w % 2 == 0:
+            current_value.append(
+                jax.lax.ppermute(current_value[-1] if current_value else local_x, row_axis, views)
+            )
+        else:
+            next_value.append(
+                jax.lax.ppermute(next_value[-1] if next_value else local_x, row_axis, row_list)
+            )
+    piece_next = jnp.stack([*current_value[::-1], local_x, *next_value], axis=0)
+    r_now = jax.lax.axis_index(row_axis) - len(current_value)
+    piece_next = piece_next[(jnp.arange(p_count) - r_now) % p_count]
+    return _update_halves(piece_next, ndim_at)
 
 
 def matmul(left, right):
@@ -79,7 +109,7 @@
     keys = matmul(inputs, key_proj).astype(jnp.bfloat16)
     values = (matmul(inputs, value_proj) + value_bias.astype(jnp.float32)).astype(jnp.bfloat16)
     all_keys, all_values, key_ids = (
-        lax.all_gather(keys, "ctx", axis=0, tiled=True),
+        turn_knots_on_mesh(keys, "ctx", 0),
         lax.all_gather(values, "ctx", axis=0, tiled=True),
         lax.all_gather(seg_local.astype(jnp.bfloat16), "ctx", axis=0, tiled=True),
     )

time: 746 us -> 745 us (level)
  waiting for transfers between devices: 438 us -> 392 us
  blocking collectives: 74.9 us -> 101 us
  local copies, waits for them, and re-layouts: 44.8 us -> 54.6 us
    all_gather x1, waiting for transfers between devices: 31.5 us -> 0.01 us  [body(): lax.all_gather(values, 'ctx', axis=0, tiled=True)]
    all_gather x1, blocking collectives: 13.7 us -> 39.5 us  [body(): lax.all_gather(seg_local.astype(jnp.bfloat16), 'ctx', axis=0, tiled=True)]
    all_gather x1 -> x0, waiting for transfers between devices: 21 us -> none  [body(): lax.all_gather(keys, 'ctx', axis=0, tiled=True)]
    ppermute x0 -> x3, waiting for transfers between devices: none -> 7.66 us  [the longest x2 7.66 us: turn_knots_on_mesh(): jax.lax.ppermute(current_value[-1] if current_value else local_x, row_axi...]
    unnamed x122 -> x120, local copies, waits for them, and re-layouts: 29.6 us -> 30 us
  transfers between devices with their start and end apart: 9 -> 11, of which waited for: 8 -> 7; matrix products, arithmetic and copies ran while one was open for 5% -> 7% of each run, Pallas kernels for 0% -> 0%
where the time goes in v1:
time: 745 us; the launch traced here: 743 us
  waiting for transfers between devices  392 us (53%)
  matrix products  140 us (19%)
  blocking collectives  101 us (14%)
  local copies, waits for them, and re-layouts  54.6 us (7%)
  other arithmetic  33.4 us (4%)
  between operations  14.7 us (2%)
    psum x1, waiting for transfers between devices, body(): lax.psum((query_grad, key_grad, value_grad, qbias_grad, vbias_grad, oproj...  231 us
    psum x1, blocking collectives, body(): lax.psum((query_grad, key_grad, value_grad, qbias_grad, vbias_grad, oproj...  61.5 us
    dot_general x24, matrix products, inner_cols(): lax.dot_general(left, right, contract_cols, preferred_element_type=jnp.fl...  52.3 us
    dot_general x18, matrix products, matmul(): return jnp.dot(left, right, preferred_element_type=jnp.float32)  47.4 us
    dot_general x18, matrix products, inner_rows(): lax.dot_general(left, right, contract_rows, preferred_element_type=jnp.fl...  40.6 us
    all_gather x1, blocking collectives, body(): lax.all_gather(seg_local.astype(jnp.bfloat16), 'ctx', axis=0, tiled=True)  39.5 us
    psum x1, waiting for transfers between devices, body(): lax.psum(matmul(hidden, shrink_proj).astype(jnp.bfloat16), 'tensor')  34.4 us
    psum x1, waiting for transfers between devices, body(): lax.psum(inner_cols(grad_pre, expand_proj).astype(jnp.bfloat16), 'tensor')  34.1 us
  transfers between devices with their start and end apart: 11, of which 7 were waited for; matrix products, arithmetic and copies ran while one was open for 7% of the time, Pallas kernels for 0%

profile of v1, /device:TPU:0, one launch (start us, length us, event | category | flops | bytes accessed | tf_op | source)
XLA Modules:
  0.0 742.7 jit_solution(14951259654134687632)
XLA Ops:
  8.1 2.7 fusion.62
  12.5 3.1 collective-permute-start
  15.6 2.1 collective-permute-start.2
  17.7 39.5 %all-gather = bf16[1,2048]{1,0:T(2,128)(2,1)S(1)} all-gather(bf16[1,512]{1,0:T(2,128)(2,1)S(1)} %get-tuple-element.288), channel_id=2, replica_groups=mesh['dp'=4,'ctx'=4,'tensor'=2] {'ctx'}, dimensions={1}, use_global_device_ids=true | all-gather | bytes 5120 | tf_op jit(solution)/shard_map/all_gather | solution.py:114
  57.3 2.3 fusion.61
  59.6 2.2 copy.42
  61.8 7.7 %collective-permute-done.1 = bf16[512,384]{1,0:T(8,128)(2,1)} collective-permute-done((bf16[512,384]{1,0:T(8,128)(2,1)}, bf16[512,384]{1,0:T(8,128)(2,1)}, u32[]{:S(2)}, u32[]{:S(2)}) %collective-permute-start.1) | collective-permute-done | bytes 393248 | tf_op jit(solution)/shard_map/ppermute | solution.py:31
  69.5 2.6 pad_maximum_fusion
  72.1 3.3 gather_fusion
  75.4 3.9 copy.43
  79.3 3.8 reshape_reshape.3
  83.1 4.1 copy.45
  87.2 2.6 copy.44
  89.7 4.1 copy.46
  93.9 38.4 %while.28 = (s32[]{:T(128)}, bf16[6,512,64]{1,2,0:T(8,128)(2,1)S(1)}, f32[6,512,1]{1,2,0:T(1,128)}, bf16[6,512,64]{2,1,0:T(8,128)(2,1)}, bf16[6,2048,64]{2,1,0:T...) while((s32[]{:T(128)}, ...), condition=%wide.region_3.4_spmd.clone, body=%wide.region_0.3_spmd.clone.sunk | while | flops 286260736 | bytes 13946985 | solution.py:141
  93.9 2.0 fusion.134
  97.1 2.6 fusion.136
  103.5 2.6 fusion.136
  109.9 2.6 fusion.136
  116.3 2.6 fusion.136
  122.7 2.6 fusion.136
  129.1 2.6 fusion.136
  132.3 2.7 convolution_convert_fusion.2
  139.7 28.9 %all-reduce.8.cloned.1.call-done = bf16[512,768]{1,0:T(8,128)(2,1)} async-done(((bf16[512,768]{1,0:T(8,128)(2,1)}), bf16[512,768]{1,0:T(8,128)(2,1)}) %all-reduce.8.cloned.1.call-update) | async-done | bytes 786448 | tf_op jit(solution)/shard_map/psum | solution.py:143
  170.7 9.5 %multiply_convert_fusion.1 = (bf16[512,1536]{1,0:T(8,128)(2,1)S(1)}, f32[512,1536]{1,0:T(8,128)}, f32[512,1536]{1,0:T(8,128)}) fusion(f32[1536]{0:T(1024)S(1)} %copy-done.41, bf16[768,1536]{1,0:T(8,128)(2,1)S(1)} %copy-done, f32[768]{0:T(1024)S(1)} %copy-done.38, f32[768]{0:T(1024)S(1)} %copy-done.23, f32[512]{0:T(512)S(1)} %add_rsqrt_fusion.1, ...), kind=kOutput, calls=%fused_computation.63 | convolution fusion | flops 1263403008 | bytes 11815936 | tf_op jit(solution)/shard_map/dot_general | solution.py:44
  181.5 2.3 convolution_convert_fusion.1
  183.9 34.4 %all-reduce.10.cloned.1.call-done = bf16[512,768]{1,0:T(8,128)(2,1)} async-done(((bf16[512,768]{1,0:T(8,128)(2,1)}), bf16[512,768]{1,0:T(8,128)(2,1)}) %all-reduce.10.cloned.1.call-update) | async-done | bytes 786448 | tf_op jit(solution)/shard_map/psum | solution.py:156
  218.3 2.2 fusion.80
  224.2 2.9 convert_reduce_fusion
  228.3 2.3 convolution_convert_fusion
  230.9 34.1 %all-reduce.12.cloned.1.call-done = bf16[512,768]{1,0:T(8,128)(2,1)} async-done(((bf16[512,768]{1,0:T(8,128)(2,1)}), bf16[512,768]{1,0:T(8,128)(2,1)}) %all-reduce.12.cloned.1.call-update) | async-done | bytes 786448 | tf_op jit(solution)/shard_map/psum | solution.py:175
  265.1 3.5 multiply_reduce_fusion.1
  272.9 69.9 %while.29 = (s32[]{:T(128)}, bf16[6,512,64]{1,2,0:T(8,128)(2,1)S(1)}, bf16[6,2048,64]{1,2,0:T(8,128)(2,1)}, bf16[6,2048,64]{1,2,0:T(8,128)(2,1)}, bf16[6,512,64]...) while((s32[]{:T(128)}, ...), condition=%wide.region_17.18_spmd.clone, body=%wide.region_15.17_spmd.clone.sunk | while | flops 681737728 | bytes 34759808 | solution.py:199
  275.4 2.6 multiply_reduce_fusion.7
  278.5 2.2 fusion.148
  282.4 2.1 fusion.147
  287.1 2.6 multiply_reduce_fusion.7
  290.1 2.1 fusion.148
  294.1 2.1 fusion.147
  298.7 2.6 multiply_reduce_fusion.7
  301.7 2.2 fusion.148
  305.7 2.1 fusion.147
  310.3 2.6 multiply_reduce_fusion.7
  313.4 2.2 fusion.148
  317.4 2.1 fusion.147
  322.0 2.6 multiply_reduce_fusion.7
  325.0 2.2 fusion.148
  329.0 2.1 fusion.147
  333.6 2.6 multiply_reduce_fusion.7
  336.7 2.2 fusion.148
  340.7 2.1 fusion.147
  344.2 5.1 fusion.67
  349.4 3.8 fusion.73
  356.5 21.8 %reduce-scatter.3.cloned.1.call-done = bf16[512,384]{0,1:T(8,128)(2,1)} async-done(((bf16[2048,384]{0,1:T(8,128)(2,1)}), bf16[512,384]{0,1:T(8,128)(2,1)}) %reduce-scatter.3.cloned.1.call-update) | async-done | bytes 393232 | tf_op jit(solution)/shard_map/reduce_scatter | solution.py:204
  378.3 3.0 fusion.84
  381.2 33.6 %reduce-scatter.5.cloned.1.call-done = bf16[512,384]{0,1:T(8,128)(2,1)} async-done(((bf16[2048,384]{0,1:T(8,128)(2,1)}), bf16[512,384]{0,1:T(8,128)(2,1)}) %reduce-scatter.5.cloned.1.call-update) | async-done | bytes 393232 | tf_op jit(solution)/shard_map/reduce_scatter | solution.py:207
  414.8 3.5 add_convert_fusion.1
  423.9 61.5 %all-reduce = (f32[384]{0:T(512)}, f32[384]{0:T(512)}, f32[768]{0:T(1024)}, f32[768]{0:T(1024)}, f32[768]{0:T(1024)}, /*index=5*/f32[1536]{0:T(1024)}, f32[768]{0:T(1024)}, f32[768]{0:T(1024)}, f32[768]{0:T(1024)}) all-reduce(f32[384]{0:T(512)S(1)} %reduce_sum.182, ...), channel_id=1, replica_groups=mesh['dp'=4,'ctx'=4,'tensor'=2] {'dp','ctx'}, use_global_device_ids=true, to_apply=%region_25.26 | all-reduce | flops 6912 | bytes 55296 | tf_op jit(solution)/shard_map/psum | solution.py:240
  485.4 2.5 convert_add_fusion
  487.9 231.2 %all-reduce.16.cloned.1.call-done = (f32[768,384]{0,1:T(8,128)}, f32[768,384]{0,1:T(8,128)}, f32[768,384]{0,1:T(8,128)}, f32[384,768]{1,0:T(8,128)}, f32[768,1536]{1,0:T(8,128)}, /*index=5*/f32[1536,768]{1,0:T(8,128)}) async-done(((f32[768,384]{0,1:T(8,128)}, f32[768,384]{0,1:T(8,128)}, f32[768,384]{0,1:T(8,128)}, f32[384,768]{1,0:T(8,128)}, f32[768,1536]{1,0:T(8,128)}, /*index=5*/f32[1536,768]{1,0:T(8,128)}), ...) | async-done | bytes 14155792 | tf_op jit(solution)/shard_map/psum | solution.py:240
  719.1 2.7 copy.50
  721.8 2.7 copy.51
  727.0 5.5 copy.92
  732.5 2.4 copy.93
  (225 shorter events, 82.9 us)
Async XLA Ops:
  7.2 163.5 %copy-start = (bf16[768,1536]{1,0:T(8,128)(2,1)S(1)}, bf16[768,1536]{1,0:T(8,128)(2,1)}, u32[]{:S(2)}) copy-start(bf16[768,1536]{1,0:T(8,128)(2,1)} %param.33) | copy-start | bytes 7077892
  7.2 3.7 copy-start.2
  7.2 80.0 %all-gather.3.cloned.1.call-start = ((), (), s32[]{:S(2)}) async-start(), calls=%async_computation.2 | async-start | bytes 1966080 | tf_op jit(solution)/shard_map/all_gather | solution.py:113
  8.1 9.6 %copy-start.47 = (bf16[384]{0:T(512)(128)(2,1)S(1)}, bf16[384]{0:T(512)(128)(2,1)}, u32[]{:S(2)}) copy-start(bf16[384]{0:T(512)(128)(2,1)} %param.27) | copy-start | bytes 2308
  8.1 9.6 %copy-start.43 = (s32[1,512]{1,0:T(1,128)S(1)}, s32[1,512]{1,0:T(1,128)}, u32[]{:S(2)}) copy-start(s32[1,512]{1,0:T(1,128)} %param.23) | copy-start | bytes 6148
  10.8 157.8 %all-reduce.8.cloned.1.call-start = ((), (), s32[]{:S(2)}) async-start(), calls=%async_computation.3 | async-start | bytes 1572864 | tf_op jit(solution)/shard_map/psum | solution.py:143
  12.5 44.7 %collective-permute-start = (bf16[512,384]{1,0:T(8,128)(2,1)S(1)}, bf16[512,384]{1,0:T(8,128)(2,1)}, u32[]{:S(2)}, u32[]{:S(2)}) collective-permute-start(bf16[512,384]{1,0:T(8,128)(2,1)S(1)} %convolution_convert_fusion.4), channel_id=1, source_target_pairs={{0,2},{2,4},{4,6},{6,0},{1,3},{3,5},{5,7},{7,1},{8,10},{10,12},{12... | collective-permute-start | bytes 1179656 | tf_op jit(solution)/shard_map/ppermute | solution.py:31
  15.6 46.2 %collective-permute-start.2 = (bf16[512,384]{1,0:T(8,128)(2,1)S(1)}, bf16[512,384]{1,0:T(8,128)(2,1)}, u32[]{:S(2)}, u32[]{:S(2)}) collective-permute-start(bf16[512,384]{1,0:T(8,128)(2,1)S(1)} %convolution_convert_fusion.4), channel_id=1, source_target_pairs={{2,0},{4,2},{6,4},{0,6},{3,1},{5,3},{7,5},{1,7},{10,8},{12,10},{14... | collective-permute-start | bytes 1179656 | tf_op jit(solution)/shard_map/ppermute | solution.py:35
  57.2 12.2 %collective-permute-start.1 = (bf16[512,384]{1,0:T(8,128)(2,1)}, bf16[512,384]{1,0:T(8,128)(2,1)}, u32[]{:S(2)}, u32[]{:S(2)}) collective-permute-start(bf16[512,384]{1,0:T(8,128)(2,1)} %collective-permute-done), channel_id=1, source_target_pairs={{0,2},{2,4},{4,6},{6,0},{1,3},{3,5},{5,7},{7,1},{8,10},{10,12},{12... | collective-permute-start | bytes 1179656 | tf_op jit(solution)/shard_map/ppermute | solution.py:31
  132.3 38.4 %copy-start.12 = (bf16[6,512,64]{1,2,0:T(8,128)(2,1)}, bf16[6,512,64]{1,2,0:T(8,128)(2,1)S(1)}, u32[]{:S(2)}) copy-start(bf16[6,512,64]{1,2,0:T(8,128)(2,1)S(1)} %get-tuple-element.109) | copy-start | bytes 1179652
  135.0 83.2 %all-reduce.10.cloned.1.call-start = ((), (), s32[]{:S(2)}) async-start(), calls=%async_computation.4 | async-start | bytes 1572864 | tf_op jit(solution)/shard_map/psum | solution.py:156
  168.6 1.6 copy-start.8
  168.6 2.1 copy-start.23
  168.6 2.1 copy-start.38
  168.6 2.1 copy-start.41
  170.2 10.1 %copy-start.26 = (f32[512]{0:T(512)}, f32[512]{0:T(512)S(1)}, u32[]{:S(2)}) copy-start(f32[512]{0:T(512)S(1)} %broadcast_multiply_fusion.5) | copy-start | bytes 6148
  170.7 9.5 %copy-start.29 = (f32[512]{0:T(512)}, f32[512]{0:T(512)S(1)}, u32[]{:S(2)}) copy-start(f32[512]{0:T(512)S(1)} %add_rsqrt_fusion.1) | copy-start | bytes 6148
  170.7 10.7 %copy-start.48 = (bf16[1536,768]{1,0:T(8,128)(2,1)S(1)}, bf16[1536,768]{1,0:T(8,128)(2,1)}, u32[]{:S(2)}) copy-start(bf16[1536,768]{1,0:T(8,128)(2,1)} %param.35) | copy-start | bytes 7077892
  180.2 1.1 copy-start.16
  181.4 2.4 copy-start.44
  181.4 2.4 copy-start.45
  181.4 2.4 copy-start.46
  181.4 36.8 %copy-start.24 = (f32[768]{0:T(1024)S(1)}, f32[768]{0:T(1024)}, u32[]{:S(2)}) copy-start(f32[768]{0:T(1024)} %convert_element_type.185) | copy-start | bytes 9220
  181.4 36.8 %copy-start.27 = (f32[512]{0:T(512)S(1)}, f32[512]{0:T(512)}, u32[]{:S(2)}) copy-start(f32[512]{0:T(512)} %copy-done.26) | copy-start | bytes 6148
  181.4 36.8 %copy-start.30 = (f32[512]{0:T(512)S(1)}, f32[512]{0:T(512)}, u32[]{:S(2)}) copy-start(f32[512]{0:T(512)} %copy-done.29) | copy-start | bytes 6148
  181.4 36.8 %copy-start.39 = (f32[768]{0:T(1024)S(1)}, f32[768]{0:T(1024)}, u32[]{:S(2)}) copy-start(f32[768]{0:T(1024)} %convert_element_type.186) | copy-start | bytes 9220
  183.7 81.3 %all-reduce.12.cloned.1.call-start = ((), (), s32[]{:S(2)}) async-start(), calls=%async_computation.5 | async-start | bytes 1572864 | tf_op jit(solution)/shard_map/psum | solution.py:175
  218.2 2.6 copy-start.14
  220.5 3.4 copy-start.53
  220.8 3.1 copy-start.52
  222.2 2.1 copy-start.49
  223.9 3.2 copy-start.3
  227.1 1.2 copy-start.50
  230.6 38.0 %copy-start.4 = (f32[512,768]{1,0:T(8,128)S(1)}, f32[512,768]{1,0:T(8,128)}, u32[]{:S(2)}) copy-start(f32[512,768]{1,0:T(8,128)} %copy-done.3) | copy-start | bytes 4718596
  230.6 38.0 %copy-start.9 = (bf16[512,768]{1,0:T(8,128)(2,1)S(1)}, bf16[512,768]{1,0:T(8,128)(2,1)}, u32[]{:S(2)}) copy-start(bf16[512,768]{1,0:T(8,128)(2,1)} %all-reduce.8.cloned.1.call-done) | copy-start | bytes 2359300
  230.7 147.6 %reduce-scatter.3.cloned.1.call-start = ((), (), s32[]{:S(2)}) async-start(), calls=%async_computation.6 | async-start | bytes 1966080 | tf_op jit(solution)/shard_map/reduce_scatter | solution.py:204
  265.1 3.6 copy-start.15
  268.7 2.5 copy-start.17
  270.0 1.1 copy-start.6
  342.8 1.4 copy-start.5
  342.8 72.0 %reduce-scatter.5.cloned.1.call-start = ((), (), s32[]{:S(2)}) async-start(), calls=%async_computation.7 | async-start | bytes 1966080 | tf_op jit(solution)/shard_map/reduce_scatter | solution.py:207
  343.4 5.9 copy-start.10
  343.4 5.9 copy-start.25
  343.4 5.9 copy-start.28
  343.4 5.9 copy-start.31
  343.4 142.0 %all-reduce.14.cloned.1.call-start = ((), (), s32[]{:S(2)}) async-start(), calls=%async_computation.8 | async-start | bytes 1572864 | tf_op jit(solution)/shard_map/psum | solution.py:223
  344.2 5.2 copy-start.40
  344.2 5.2 copy-start.51
  349.4 3.9 copy-start.22
  353.2 1.8 copy-start.7
  353.2 1.8 copy-start.13
  356.5 58.3 %copy-start.21 = (bf16[768,384]{1,0:T(8,128)(2,1)S(1)}, bf16[768,384]{1,0:T(8,128)(2,1)}, u32[]{:S(2)}) copy-start(bf16[768,384]{1,0:T(8,128)(2,1)} %param.26) | copy-start | bytes 1769476
  418.3 1.8 copy-start.11
  418.4 3.3 copy-start.18
  418.4 300.7 %all-reduce.16.cloned.1.call-start = ((), (), s32[]{:S(2)}) async-start(), calls=%async_computation.9 | async-start | bytes 28311552 | tf_op jit(solution)/shard_map/psum | solution.py:240
  423.2 0.7 copy-start.35
  423.2 0.7 copy-start.36
  423.2 0.7 copy-start.37
  423.2 0.7 copy-start.42
  719.1 5.5 copy-start.20
  721.8 4.1 copy-start.19
  725.9 6.5 slice-start
  727.0 5.5 slice-start.1
  732.5 3.4 copy-start.1
  (3 other events, 2.1 us)
Sparse Core Ops, SparseCore 0:
  10.9 50.6 all-gather.2
  135.1 33.4 all-reduce.7
  183.9 34.3 all-reduce.9
  230.7 34.2 all-reduce.11
  342.9 35.2 reduce-scatter.2
  380.5 34.2 reduce-scatter.4
  418.5 33.2 all-reduce.13
  458.1 260.8 all-reduce.15
